TPU v7x, 256 devices: a whole 4x4x8 slice. The times are simulated.
256 devices in a mesh: blk: 8 (over x_hi, y), group: 32 (over z, x_lo, core).
Axes of the slice: x: 4 (x_hi: 2, x_lo: 2; x = x_hi * 2 + x_lo), y: 4, z: 8, core: 2. Of those that a mesh axis runs over, the one named last changes fastest.
Arguments:
- walk_rows: bfloat16 [4096, 131072], P('blk', 'group'), may hold values from -6 to 6
- col_values: bfloat16 [49152, 4096], P('group', 'blk'), may hold values from -0.02734375 to 0.02734375
- col_index: int32 [96, 8], P('group'), may hold values from 0 to 7
- col_count: int32 [32, 8], P('group'), may hold values from 1 to 3, as said below
Outputs:
- inflated: float32 [4096, 4096], P(('blk', 'group'))
Inputs may be any that keep to these rules, and one draw needn't show every extreme that they name: `col_count`: each list holds 1 to 3 valid slots; some list holds 3; contents of the other slots are arbitrary.
All inputs are finite; a program needn't handle non-finite values.
Results may differ from a plain program's by a relative error of at most 0.0003.
Values may be sent and summed in bfloat16 or wider, within the bound.
No kernel may reach another device: no remote copies, remote signals or barrier semaphores. Data moves between devices by JAX's collectives and lax.ppermute only.
A program may use at most 64 MiB of HBM per device.

v0:
```python
import jax
import jax.numpy as jnp
from jax import lax
from jax.sharding import PartitionSpec as P


def shifted(shard, axis, by):
    size = lax.axis_size(axis)
    return lax.ppermute(shard, axis, [(i, (i + by) % size) for i in range(size)])


def on_device(walk_rows, col_values, col_index, col_count):
    width = col_values.shape[1]
    slots = col_values.shape[0] // width
    nblock = lax.axis_size("blk")
    myself = lax.axis_index("blk")
    rows_here = walk_rows.shape[0]
    share = rows_here // lax.axis_size("group")

    def panel_product(rows, values, panel):
        index = lax.dynamic_slice_in_dim(col_index, panel, 1, 1)[:, 0]
        count = lax.dynamic_slice_in_dim(col_count, panel, 1, 1)[0, 0]
        total = jnp.zeros((rows.shape[0], width), jnp.float32)
        for slot in range(slots):
            block = lax.dynamic_slice_in_dim(rows, index[slot] * width, width, 1)
            piece = values[slot * width : (slot + 1) * width]
            product = jnp.dot(block, piece, preferred_element_type=jnp.float32)
            total = total + jnp.where(slot < count, product, jnp.zeros_like(product))
        return total

    def turn(step, carry):
        values, result = carry
        panel = (myself - step) % nblock
        part = panel_product(walk_rows, values, panel)
        reduced = lax.psum_scatter(part, "group", scatter_dimension=0, tiled=True)
        result = lax.dynamic_update_slice_in_dim(result, reduced, panel * width, 1)
        values = shifted(values, "blk", 1)
        return (values, result)

    start_out = jnp.zeros((share, nblock * width), jnp.float32)
    unused, expanded = lax.fori_loop(0, nblock, turn, (col_values, start_out))
    squared = expanded * expanded
    column = jnp.sum(squared, axis=0)
    total = lax.psum(column, ("blk", "group"))
    scale = total / (nblock * rows_here) + 1e-06
    return squared / scale


def solution(mesh):
    return jax.shard_map(
        on_device,
        mesh=mesh,
        in_specs=(P("blk", "group"), P("group", "blk"), P("group", None), P("group", None)),
        out_specs=P(("blk", "group"), None),
        check_vma=False,
    )
```

profile of v0, /device:TPU:1, one launch (start us, length us, event | category | flops | bytes accessed | tf_op | source)
XLA Modules:
  0.0 1125.3 jit_solution(7067308069750690020)
XLA Ops:
  6.6 1.4 copy-done
  7.9 1030.1 %while.17 = (s32[]{:T(128)}, bf16[1536,512]{1,0:T(8,128)(2,1)S(1)}, f32[16,4096]{1,0:T(8,128)S(1)}, s32[]{:T(128)}, s32[1,8]{1,0:T(1,128)S(1)}, /*index=5*/s32[3...) while((s32[]{:T(128)}, bf16[1536,512]{1,0:T(8,128)(2,1)S(1)}, ...), condition=%wide.region_2.3_spmd, body=%wide.region_0.2_spmd.sunk | while | flops 806617088 | bytes 21137560 | solution.py:41
  8.1 0.6 fusion.28
  10.5 0.7 fusion.29
  12.4 2.1 convolution_select_fusion.5
  14.5 1.5 convolution_select_fusion.6
  16.0 2.5 fusion.30
  18.5 2.2 collective-permute-start
  20.7 117.8 %reduce-scatter.2.cloned.1.call-done = f32[16,512]{1,0:T(8,128)} async-done(((f32[512,512]{1,0:T(8,128)}), f32[16,512]{1,0:T(8,128)}) %reduce-scatter.2.cloned.1.call-update) | async-done | bytes 32784 | tf_op jit(solution)/shard_map/while/body/eval_jaxpr/reduce_scatter | solution.py:35
  138.5 0.8 constant_dynamic-update-slice_fusion.2
  139.4 0.6 fusion.28
  141.8 0.7 fusion.29
  143.7 2.1 convolution_select_fusion.5
  145.8 1.5 convolution_select_fusion.6
  147.3 2.5 fusion.30
  149.9 117.1 %reduce-scatter.2.cloned.1.call-done = f32[16,512]{1,0:T(8,128)} async-done(((f32[512,512]{1,0:T(8,128)}), f32[16,512]{1,0:T(8,128)}) %reduce-scatter.2.cloned.1.call-update) | async-done | bytes 32784 | tf_op jit(solution)/shard_map/while/body/eval_jaxpr/reduce_scatter | solution.py:35
  267.0 0.8 constant_dynamic-update-slice_fusion.2
  267.8 0.6 fusion.28
  270.3 0.7 fusion.29
  272.2 2.1 convolution_select_fusion.5
  274.3 1.5 convolution_select_fusion.6
  275.8 2.5 fusion.30
  278.4 116.7 %reduce-scatter.2.cloned.1.call-done = f32[16,512]{1,0:T(8,128)} async-done(((f32[512,512]{1,0:T(8,128)}), f32[16,512]{1,0:T(8,128)}) %reduce-scatter.2.cloned.1.call-update) | async-done | bytes 32784 | tf_op jit(solution)/shard_map/while/body/eval_jaxpr/reduce_scatter | solution.py:35
  395.1 0.8 constant_dynamic-update-slice_fusion.2
  396.0 0.6 fusion.28
  398.4 0.7 fusion.29
  400.4 2.1 convolution_select_fusion.5
  402.5 1.5 convolution_select_fusion.6
  404.0 2.5 fusion.30
  406.6 116.8 %reduce-scatter.2.cloned.1.call-done = f32[16,512]{1,0:T(8,128)} async-done(((f32[512,512]{1,0:T(8,128)}), f32[16,512]{1,0:T(8,128)}) %reduce-scatter.2.cloned.1.call-update) | async-done | bytes 32784 | tf_op jit(solution)/shard_map/while/body/eval_jaxpr/reduce_scatter | solution.py:35
  523.4 0.8 constant_dynamic-update-slice_fusion.2
  524.3 0.6 fusion.28
  526.8 0.7 fusion.29
  528.7 2.1 convolution_select_fusion.5
  530.8 1.5 convolution_select_fusion.6
  532.3 2.5 fusion.30
  535.0 116.8 %reduce-scatter.2.cloned.1.call-done = f32[16,512]{1,0:T(8,128)} async-done(((f32[512,512]{1,0:T(8,128)}), f32[16,512]{1,0:T(8,128)}) %reduce-scatter.2.cloned.1.call-update) | async-done | bytes 32784 | tf_op jit(solution)/shard_map/while/body/eval_jaxpr/reduce_scatter | solution.py:35
  651.9 0.8 constant_dynamic-update-slice_fusion.2
  652.7 0.6 fusion.28
  655.2 0.7 fusion.29
  657.1 2.1 convolution_select_fusion.5
  659.2 1.5 convolution_select_fusion.6
  660.7 2.5 fusion.30
  663.2 0.3 collective-permute-start
  663.5 116.9 %reduce-scatter.2.cloned.1.call-done = f32[16,512]{1,0:T(8,128)} async-done(((f32[512,512]{1,0:T(8,128)}), f32[16,512]{1,0:T(8,128)}) %reduce-scatter.2.cloned.1.call-update) | async-done | bytes 32784 | tf_op jit(solution)/shard_map/while/body/eval_jaxpr/reduce_scatter | solution.py:35
  780.3 0.8 constant_dynamic-update-slice_fusion.2
  781.2 0.6 fusion.28
  783.7 0.7 fusion.29
  785.6 2.1 convolution_select_fusion.5
  787.7 1.5 convolution_select_fusion.6
  789.2 2.5 fusion.30
  791.7 0.3 collective-permute-start
  791.9 116.9 %reduce-scatter.2.cloned.1.call-done = f32[16,512]{1,0:T(8,128)} async-done(((f32[512,512]{1,0:T(8,128)}), f32[16,512]{1,0:T(8,128)}) %reduce-scatter.2.cloned.1.call-update) | async-done | bytes 32784 | tf_op jit(solution)/shard_map/while/body/eval_jaxpr/reduce_scatter | solution.py:35
  908.8 0.8 constant_dynamic-update-slice_fusion.2
  909.7 0.6 fusion.28
  912.1 0.7 fusion.29
  914.0 2.1 convolution_select_fusion.5
  916.1 1.5 convolution_select_fusion.6
  917.6 2.5 fusion.30
  920.1 0.5 collective-permute-start
  920.6 116.6 %reduce-scatter.2.cloned.1.call-done = f32[16,512]{1,0:T(8,128)} async-done(((f32[512,512]{1,0:T(8,128)}), f32[16,512]{1,0:T(8,128)}) %reduce-scatter.2.cloned.1.call-update) | async-done | bytes 32784 | tf_op jit(solution)/shard_map/while/body/eval_jaxpr/reduce_scatter | solution.py:35
  1037.3 0.8 constant_dynamic-update-slice_fusion.2
  1038.1 79.7 %psum.7 = f32[4096]{0:T(1024)S(1)} all-reduce(f32[4096]{0:T(1024)S(1)} %multiply_reduce_fusion), channel_id=1, replica_groups=mesh['blk'=8,'group'=32] {'blk','group'}, use_global_device_ids=true, to_apply=%region_4.5 | all-reduce | flops 4096 | bytes 32768 | tf_op jit(solution)/shard_map/psum | solution.py:44
  1117.7 0.7 multiply_divide_fusion
  (52 shorter events, 2.3 us)
Async XLA Ops:
  6.5 1.4 copy-start
  6.5 1.4 copy-start.1
  6.5 1.4 copy-start.2
  7.9 130.5 %reduce-scatter.2.cloned.1.call-start = ((), (), s32[]{:S(2)}) async-start(), calls=%async_computation.1 | async-start | bytes 1081344 | tf_op jit(solution)/shard_map/while/body/eval_jaxpr/reduce_scatter | solution.py:35
  18.5 120.8 %collective-permute-start = (bf16[1536,512]{1,0:T(8,128)(2,1)S(1)}, bf16[1536,512]{1,0:T(8,128)(2,1)S(1)}, u32[]{:S(2)}, u32[]{:S(2)}) collective-permute-start(bf16[1536,512]{1,0:T(8,128)(2,1)S(1)} %copy.10), channel_id=1, source_target_pairs={{0,32},{32,64},{64,96},{96,128},{128,160},{160,192},{192,224},{224... | collective-permute-start | bytes 4718600 | tf_op jit(solution)/shard_map/while/body/eval_jaxpr/ppermute | solution.py:9
  139.3 127.7 %reduce-scatter.2.cloned.1.call-start = ((), (), s32[]{:S(2)}) async-start(), calls=%async_computation.1 | async-start | bytes 1081344 | tf_op jit(solution)/shard_map/while/body/eval_jaxpr/reduce_scatter | solution.py:35
  149.8 117.9 %collective-permute-start = (bf16[1536,512]{1,0:T(8,128)(2,1)S(1)}, bf16[1536,512]{1,0:T(8,128)(2,1)S(1)}, u32[]{:S(2)}, u32[]{:S(2)}) collective-permute-start(bf16[1536,512]{1,0:T(8,128)(2,1)S(1)} %copy.10), channel_id=1, source_target_pairs={{0,32},{32,64},{64,96},{96,128},{128,160},{160,192},{192,224},{224... | collective-permute-start | bytes 4718600 | tf_op jit(solution)/shard_map/while/body/eval_jaxpr/ppermute | solution.py:9
  267.7 127.4 %reduce-scatter.2.cloned.1.call-start = ((), (), s32[]{:S(2)}) async-start(), calls=%async_computation.1 | async-start | bytes 1081344 | tf_op jit(solution)/shard_map/while/body/eval_jaxpr/reduce_scatter | solution.py:35
  278.3 117.6 %collective-permute-start = (bf16[1536,512]{1,0:T(8,128)(2,1)S(1)}, bf16[1536,512]{1,0:T(8,128)(2,1)S(1)}, u32[]{:S(2)}, u32[]{:S(2)}) collective-permute-start(bf16[1536,512]{1,0:T(8,128)(2,1)S(1)} %copy.10), channel_id=1, source_target_pairs={{0,32},{32,64},{64,96},{96,128},{128,160},{160,192},{192,224},{224... | collective-permute-start | bytes 4718600 | tf_op jit(solution)/shard_map/while/body/eval_jaxpr/ppermute | solution.py:9
  395.9 127.5 %reduce-scatter.2.cloned.1.call-start = ((), (), s32[]{:S(2)}) async-start(), calls=%async_computation.1 | async-start | bytes 1081344 | tf_op jit(solution)/shard_map/while/body/eval_jaxpr/reduce_scatter | solution.py:35
  406.4 117.8 %collective-permute-start = (bf16[1536,512]{1,0:T(8,128)(2,1)S(1)}, bf16[1536,512]{1,0:T(8,128)(2,1)S(1)}, u32[]{:S(2)}, u32[]{:S(2)}) collective-permute-start(bf16[1536,512]{1,0:T(8,128)(2,1)S(1)} %copy.10), channel_id=1, source_target_pairs={{0,32},{32,64},{64,96},{96,128},{128,160},{160,192},{192,224},{224... | collective-permute-start | bytes 4718600 | tf_op jit(solution)/shard_map/while/body/eval_jaxpr/ppermute | solution.py:9
  524.2 127.7 %reduce-scatter.2.cloned.1.call-start = ((), (), s32[]{:S(2)}) async-start(), calls=%async_computation.1 | async-start | bytes 1081344 | tf_op jit(solution)/shard_map/while/body/eval_jaxpr/reduce_scatter | solution.py:35
  534.8 117.9 %collective-permute-start = (bf16[1536,512]{1,0:T(8,128)(2,1)S(1)}, bf16[1536,512]{1,0:T(8,128)(2,1)S(1)}, u32[]{:S(2)}, u32[]{:S(2)}) collective-permute-start(bf16[1536,512]{1,0:T(8,128)(2,1)S(1)} %copy.10), channel_id=1, source_target_pairs={{0,32},{32,64},{64,96},{96,128},{128,160},{160,192},{192,224},{224... | collective-permute-start | bytes 4718600 | tf_op jit(solution)/shard_map/while/body/eval_jaxpr/ppermute | solution.py:9
  652.6 127.7 %reduce-scatter.2.cloned.1.call-start = ((), (), s32[]{:S(2)}) async-start(), calls=%async_computation.1 | async-start | bytes 1081344 | tf_op jit(solution)/shard_map/while/body/eval_jaxpr/reduce_scatter | solution.py:35
  663.2 117.9 %collective-permute-start = (bf16[1536,512]{1,0:T(8,128)(2,1)S(1)}, bf16[1536,512]{1,0:T(8,128)(2,1)S(1)}, u32[]{:S(2)}, u32[]{:S(2)}) collective-permute-start(bf16[1536,512]{1,0:T(8,128)(2,1)S(1)} %copy.10), channel_id=1, source_target_pairs={{0,32},{32,64},{64,96},{96,128},{128,160},{160,192},{192,224},{224... | collective-permute-start | bytes 4718600 | tf_op jit(solution)/shard_map/while/body/eval_jaxpr/ppermute | solution.py:9
  781.1 127.7 %reduce-scatter.2.cloned.1.call-start = ((), (), s32[]{:S(2)}) async-start(), calls=%async_computation.1 | async-start | bytes 1081344 | tf_op jit(solution)/shard_map/while/body/eval_jaxpr/reduce_scatter | solution.py:35
  791.7 117.9 %collective-permute-start = (bf16[1536,512]{1,0:T(8,128)(2,1)S(1)}, bf16[1536,512]{1,0:T(8,128)(2,1)S(1)}, u32[]{:S(2)}, u32[]{:S(2)}) collective-permute-start(bf16[1536,512]{1,0:T(8,128)(2,1)S(1)} %copy.10), channel_id=1, source_target_pairs={{0,32},{32,64},{64,96},{96,128},{128,160},{160,192},{192,224},{224... | collective-permute-start | bytes 4718600 | tf_op jit(solution)/shard_map/while/body/eval_jaxpr/ppermute | solution.py:9
  909.6 127.7 %reduce-scatter.2.cloned.1.call-start = ((), (), s32[]{:S(2)}) async-start(), calls=%async_computation.1 | async-start | bytes 1081344 | tf_op jit(solution)/shard_map/while/body/eval_jaxpr/reduce_scatter | solution.py:35
  920.1 117.9 %collective-permute-start = (bf16[1536,512]{1,0:T(8,128)(2,1)S(1)}, bf16[1536,512]{1,0:T(8,128)(2,1)S(1)}, u32[]{:S(2)}, u32[]{:S(2)}) collective-permute-start(bf16[1536,512]{1,0:T(8,128)(2,1)S(1)} %copy.10), channel_id=1, source_target_pairs={{0,32},{32,64},{64,96},{96,128},{128,160},{160,192},{192,224},{224... | collective-permute-start | bytes 4718600 | tf_op jit(solution)/shard_map/while/body/eval_jaxpr/ppermute | solution.py:9
Sparse Core Ops, SparseCore 0:
  18.6 119.8 reduce-scatter.1
  149.9 116.9 reduce-scatter.1
  278.4 116.6 reduce-scatter.1
  406.6 116.8 reduce-scatter.1
  534.9 116.9 reduce-scatter.1
  663.3 116.9 reduce-scatter.1
  791.8 116.9 reduce-scatter.1
  920.2 116.9 reduce-scatter.1
where the time goes:
time: 1130 us
  waiting for transfers between devices  936 us (83%)
  blocking collectives  79.7 us (7%)
  matrix products  48.4 us (4%)
  loops' own time  24.6 us (2%)
  local copies, waits for them, and re-layouts  13.6 us (1%)
  between operations  13.4 us (1%)
    reduce_scatter x8, waiting for transfers between devices, turn(): reduced = lax.psum_scatter(part, 'group', scatter_dimension=0, tiled=True)  936 us
    psum x1, blocking collectives, on_device(): total = lax.psum(column, ('blk', 'group'))  79.7 us
    dot_general x24, matrix products, panel_product(): product = jnp.dot(block, piece, preferred_element_type=jnp.float32)  48.4 us
    another operation x1, loops' own time, on_device(): unused, expanded = lax.fori_loop(0, nblock, turn, (col_values, start_out))  24.6 us
  transfers between devices with their start and end apart: 16, of which 8 were waited for; matrix products, arithmetic and copies ran while one was open for 1% of the time, Pallas kernels for 0%

commit v1 on v0

--- a/solution.py
+++ b/solution.py
@@ -41,7 +41,7 @@
     unused, expanded = lax.fori_loop(0, nblock, turn, (col_values, start_out))
     squared = expanded * expanded
     column = jnp.sum(squared, axis=0)
-    total = lax.psum(column, ("blk", "group"))
+    total = lax.psum(lax.psum(column, "blk"), "group")
     scale = total / (nblock * rows_here) + 1e-06
     return squared / scale
 

time: 1130 us -> 1190 us (1.053)
  blocking collectives: 79.7 us -> 146 us
    psum x1 -> x2, blocking collectives: 79.7 us -> 146 us  [on_device(): total = lax.psum(lax.psum(column, 'blk'), 'group')]
where the time goes in v1:
time: 1190 us
  waiting for transfers between devices  935 us (79%)
  blocking collectives  146 us (12%)
  matrix products  48 us (4%)
  loops' own time  25.2 us (2%)
  local copies, waits for them, and re-layouts  13.6 us (1%)
  between operations  13.4 us (1%)
    reduce_scatter x8, waiting for transfers between devices, turn(): reduced = lax.psum_scatter(part, 'group', scatter_dimension=0, tiled=True)  935 us
    psum x2, blocking collectives, on_device(): total = lax.psum(lax.psum(column, 'blk'), 'group')  146 us
    dot_general x24, matrix products, panel_product(): product = jnp.dot(block, piece, preferred_element_type=jnp.float32)  48 us
    another operation x1, loops' own time, on_device(): unused, expanded = lax.fori_loop(0, nblock, turn, (col_values, start_out))  25.2 us
  transfers between devices with their start and end apart: 16, of which 8 were waited for; matrix products, arithmetic and copies ran while one was open for 1% of the time, Pallas kernels for 0%

profile of v1, /device:TPU:1, one launch (start us, length us, event | category | flops | bytes accessed | tf_op | source)
XLA Modules:
  0.0 1190.7 jit_solution(7623201862333923885)
XLA Ops:
  6.6 1.4 copy-done
  7.9 1029.5 %while.17 = (s32[]{:T(128)}, bf16[1536,512]{1,0:T(8,128)(2,1)S(1)}, f32[16,4096]{1,0:T(8,128)S(1)}, s32[]{:T(128)}, s32[1,8]{1,0:T(1,128)S(1)}, /*index=5*/s32[3...) while((s32[]{:T(128)}, bf16[1536,512]{1,0:T(8,128)(2,1)S(1)}, ...), condition=%wide.region_2.3_spmd, body=%wide.region_0.2_spmd.sunk | while | flops 806617088 | bytes 21137560 | solution.py:41
  8.1 0.6 fusion.28
  10.5 0.6 fusion.29
  12.4 2.0 convolution_select_fusion.5
  14.5 1.5 convolution_select_fusion.6
  16.0 2.5 fusion.30
  18.5 2.2 collective-permute-start
  20.7 117.8 %reduce-scatter.2.cloned.1.call-done = f32[16,512]{1,0:T(8,128)} async-done(((f32[512,512]{1,0:T(8,128)}), f32[16,512]{1,0:T(8,128)}) %reduce-scatter.2.cloned.1.call-update) | async-done | bytes 32784 | tf_op jit(solution)/shard_map/while/body/eval_jaxpr/reduce_scatter | solution.py:35
  138.5 0.8 constant_dynamic-update-slice_fusion.2
  139.3 0.6 fusion.28
  141.8 0.6 fusion.29
  143.7 2.0 convolution_select_fusion.5
  145.8 1.5 convolution_select_fusion.6
  147.3 2.5 fusion.30
  149.9 117.0 %reduce-scatter.2.cloned.1.call-done = f32[16,512]{1,0:T(8,128)} async-done(((f32[512,512]{1,0:T(8,128)}), f32[16,512]{1,0:T(8,128)}) %reduce-scatter.2.cloned.1.call-update) | async-done | bytes 32784 | tf_op jit(solution)/shard_map/while/body/eval_jaxpr/reduce_scatter | solution.py:35
  266.9 0.8 constant_dynamic-update-slice_fusion.2
  267.8 0.6 fusion.28
  270.2 0.6 fusion.29
  272.2 2.0 convolution_select_fusion.5
  274.2 1.5 convolution_select_fusion.6
  275.7 2.5 fusion.30
  278.3 117.0 %reduce-scatter.2.cloned.1.call-done = f32[16,512]{1,0:T(8,128)} async-done(((f32[512,512]{1,0:T(8,128)}), f32[16,512]{1,0:T(8,128)}) %reduce-scatter.2.cloned.1.call-update) | async-done | bytes 32784 | tf_op jit(solution)/shard_map/while/body/eval_jaxpr/reduce_scatter | solution.py:35
  395.3 0.8 constant_dynamic-update-slice_fusion.2
  396.2 0.6 fusion.28
  398.6 0.6 fusion.29
  400.6 2.0 convolution_select_fusion.5
  402.6 1.5 convolution_select_fusion.6
  404.1 2.5 fusion.30
  406.7 116.7 %reduce-scatter.2.cloned.1.call-done = f32[16,512]{1,0:T(8,128)} async-done(((f32[512,512]{1,0:T(8,128)}), f32[16,512]{1,0:T(8,128)}) %reduce-scatter.2.cloned.1.call-update) | async-done | bytes 32784 | tf_op jit(solution)/shard_map/while/body/eval_jaxpr/reduce_scatter | solution.py:35
  523.4 0.8 constant_dynamic-update-slice_fusion.2
  524.3 0.6 fusion.28
  526.7 0.6 fusion.29
  528.7 2.0 convolution_select_fusion.5
  530.7 1.5 convolution_select_fusion.6
  532.2 2.5 fusion.30
  535.0 116.8 %reduce-scatter.2.cloned.1.call-done = f32[16,512]{1,0:T(8,128)} async-done(((f32[512,512]{1,0:T(8,128)}), f32[16,512]{1,0:T(8,128)}) %reduce-scatter.2.cloned.1.call-update) | async-done | bytes 32784 | tf_op jit(solution)/shard_map/while/body/eval_jaxpr/reduce_scatter | solution.py:35
  651.8 0.8 constant_dynamic-update-slice_fusion.2
  652.7 0.6 fusion.28
  655.1 0.6 fusion.29
  657.0 2.0 convolution_select_fusion.5
  659.1 1.5 convolution_select_fusion.6
  660.6 2.5 fusion.30
  663.3 117.0 %reduce-scatter.2.cloned.1.call-done = f32[16,512]{1,0:T(8,128)} async-done(((f32[512,512]{1,0:T(8,128)}), f32[16,512]{1,0:T(8,128)}) %reduce-scatter.2.cloned.1.call-update) | async-done | bytes 32784 | tf_op jit(solution)/shard_map/while/body/eval_jaxpr/reduce_scatter | solution.py:35
  780.3 0.8 constant_dynamic-update-slice_fusion.2
  781.2 0.6 fusion.28
  783.6 0.6 fusion.29
  785.6 2.0 convolution_select_fusion.5
  787.6 1.5 convolution_select_fusion.6
  789.1 2.5 fusion.30
  791.6 0.4 collective-permute-start
  792.0 116.5 %reduce-scatter.2.cloned.1.call-done = f32[16,512]{1,0:T(8,128)} async-done(((f32[512,512]{1,0:T(8,128)}), f32[16,512]{1,0:T(8,128)}) %reduce-scatter.2.cloned.1.call-update) | async-done | bytes 32784 | tf_op jit(solution)/shard_map/while/body/eval_jaxpr/reduce_scatter | solution.py:35
  908.5 0.8 constant_dynamic-update-slice_fusion.2
  909.4 0.6 fusion.28
  911.8 0.6 fusion.29
  913.8 2.0 convolution_select_fusion.5
  915.8 1.5 convolution_select_fusion.6
  917.3 2.5 fusion.30
  919.8 0.3 collective-permute-start
  920.2 116.5 %reduce-scatter.2.cloned.1.call-done = f32[16,512]{1,0:T(8,128)} async-done(((f32[512,512]{1,0:T(8,128)}), f32[16,512]{1,0:T(8,128)}) %reduce-scatter.2.cloned.1.call-update) | async-done | bytes 32784 | tf_op jit(solution)/shard_map/while/body/eval_jaxpr/reduce_scatter | solution.py:35
  1036.7 0.8 constant_dynamic-update-slice_fusion.2
  1037.5 34.3 %psum.14 = f32[4096]{0:T(1024)S(1)} all-reduce(f32[4096]{0:T(1024)S(1)} %multiply_reduce_fusion), channel_id=1, replica_groups=mesh['blk'=8,'group'=32] {'blk'}, use_global_device_ids=true, to_apply=%region_4.5 | all-reduce | flops 4096 | bytes 32768 | tf_op jit(solution)/shard_map/psum | solution.py:44
  1071.8 111.3 %psum.15 = f32[4096]{0:T(1024)S(1)} all-reduce(f32[4096]{0:T(1024)S(1)} %psum.14), channel_id=1, replica_groups=mesh['blk'=8,'group'=32] {'group'}, use_global_device_ids=true, to_apply=%region_5.6 | all-reduce | flops 4096 | bytes 32768 | tf_op jit(solution)/shard_map/psum | solution.py:44
  1183.2 0.7 multiply_divide_fusion
  (53 shorter events, 2.4 us)
Async XLA Ops:
  6.5 1.4 copy-start
  6.5 1.4 copy-start.1
  6.5 1.4 copy-start.2
  7.9 130.5 %reduce-scatter.2.cloned.1.call-start = ((), (), s32[]{:S(2)}) async-start(), calls=%async_computation.1 | async-start | bytes 1081344 | tf_op jit(solution)/shard_map/while/body/eval_jaxpr/reduce_scatter | solution.py:35
  18.5 120.8 %collective-permute-start = (bf16[1536,512]{1,0:T(8,128)(2,1)S(1)}, bf16[1536,512]{1,0:T(8,128)(2,1)S(1)}, u32[]{:S(2)}, u32[]{:S(2)}) collective-permute-start(bf16[1536,512]{1,0:T(8,128)(2,1)S(1)} %copy.10), channel_id=1, source_target_pairs={{0,32},{32,64},{64,96},{96,128},{128,160},{160,192},{192,224},{224... | collective-permute-start | bytes 4718600 | tf_op jit(solution)/shard_map/while/body/eval_jaxpr/ppermute | solution.py:9
  139.2 127.7 %reduce-scatter.2.cloned.1.call-start = ((), (), s32[]{:S(2)}) async-start(), calls=%async_computation.1 | async-start | bytes 1081344 | tf_op jit(solution)/shard_map/while/body/eval_jaxpr/reduce_scatter | solution.py:35
  149.8 117.9 %collective-permute-start = (bf16[1536,512]{1,0:T(8,128)(2,1)S(1)}, bf16[1536,512]{1,0:T(8,128)(2,1)S(1)}, u32[]{:S(2)}, u32[]{:S(2)}) collective-permute-start(bf16[1536,512]{1,0:T(8,128)(2,1)S(1)} %copy.10), channel_id=1, source_target_pairs={{0,32},{32,64},{64,96},{96,128},{128,160},{160,192},{192,224},{224... | collective-permute-start | bytes 4718600 | tf_op jit(solution)/shard_map/while/body/eval_jaxpr/ppermute | solution.py:9
  267.7 127.7 %reduce-scatter.2.cloned.1.call-start = ((), (), s32[]{:S(2)}) async-start(), calls=%async_computation.1 | async-start | bytes 1081344 | tf_op jit(solution)/shard_map/while/body/eval_jaxpr/reduce_scatter | solution.py:35
  278.2 117.9 %collective-permute-start = (bf16[1536,512]{1,0:T(8,128)(2,1)S(1)}, bf16[1536,512]{1,0:T(8,128)(2,1)S(1)}, u32[]{:S(2)}, u32[]{:S(2)}) collective-permute-start(bf16[1536,512]{1,0:T(8,128)(2,1)S(1)} %copy.10), channel_id=1, source_target_pairs={{0,32},{32,64},{64,96},{96,128},{128,160},{160,192},{192,224},{224... | collective-permute-start | bytes 4718600 | tf_op jit(solution)/shard_map/while/body/eval_jaxpr/ppermute | solution.py:9
  396.1 127.3 %reduce-scatter.2.cloned.1.call-start = ((), (), s32[]{:S(2)}) async-start(), calls=%async_computation.1 | async-start | bytes 1081344 | tf_op jit(solution)/shard_map/while/body/eval_jaxpr/reduce_scatter | solution.py:35
  406.6 117.6 %collective-permute-start = (bf16[1536,512]{1,0:T(8,128)(2,1)S(1)}, bf16[1536,512]{1,0:T(8,128)(2,1)S(1)}, u32[]{:S(2)}, u32[]{:S(2)}) collective-permute-start(bf16[1536,512]{1,0:T(8,128)(2,1)S(1)} %copy.10), channel_id=1, source_target_pairs={{0,32},{32,64},{64,96},{96,128},{128,160},{160,192},{192,224},{224... | collective-permute-start | bytes 4718600 | tf_op jit(solution)/shard_map/while/body/eval_jaxpr/ppermute | solution.py:9
  524.2 127.6 %reduce-scatter.2.cloned.1.call-start = ((), (), s32[]{:S(2)}) async-start(), calls=%async_computation.1 | async-start | bytes 1081344 | tf_op jit(solution)/shard_map/while/body/eval_jaxpr/reduce_scatter | solution.py:35
  534.7 117.8 %collective-permute-start = (bf16[1536,512]{1,0:T(8,128)(2,1)S(1)}, bf16[1536,512]{1,0:T(8,128)(2,1)S(1)}, u32[]{:S(2)}, u32[]{:S(2)}) collective-permute-start(bf16[1536,512]{1,0:T(8,128)(2,1)S(1)} %copy.10), channel_id=1, source_target_pairs={{0,32},{32,64},{64,96},{96,128},{128,160},{160,192},{192,224},{224... | collective-permute-start | bytes 4718600 | tf_op jit(solution)/shard_map/while/body/eval_jaxpr/ppermute | solution.py:9
  652.5 127.7 %reduce-scatter.2.cloned.1.call-start = ((), (), s32[]{:S(2)}) async-start(), calls=%async_computation.1 | async-start | bytes 1081344 | tf_op jit(solution)/shard_map/while/body/eval_jaxpr/reduce_scatter | solution.py:35
  663.1 118.0 %collective-permute-start = (bf16[1536,512]{1,0:T(8,128)(2,1)S(1)}, bf16[1536,512]{1,0:T(8,128)(2,1)S(1)}, u32[]{:S(2)}, u32[]{:S(2)}) collective-permute-start(bf16[1536,512]{1,0:T(8,128)(2,1)S(1)} %copy.10), channel_id=1, source_target_pairs={{0,32},{32,64},{64,96},{96,128},{128,160},{160,192},{192,224},{224... | collective-permute-start | bytes 4718600 | tf_op jit(solution)/shard_map/while/body/eval_jaxpr/ppermute | solution.py:9
  781.1 127.5 %reduce-scatter.2.cloned.1.call-start = ((), (), s32[]{:S(2)}) async-start(), calls=%async_computation.1 | async-start | bytes 1081344 | tf_op jit(solution)/shard_map/while/body/eval_jaxpr/reduce_scatter | solution.py:35
  791.6 117.7 %collective-permute-start = (bf16[1536,512]{1,0:T(8,128)(2,1)S(1)}, bf16[1536,512]{1,0:T(8,128)(2,1)S(1)}, u32[]{:S(2)}, u32[]{:S(2)}) collective-permute-start(bf16[1536,512]{1,0:T(8,128)(2,1)S(1)} %copy.10), channel_id=1, source_target_pairs={{0,32},{32,64},{64,96},{96,128},{128,160},{160,192},{192,224},{224... | collective-permute-start | bytes 4718600 | tf_op jit(solution)/shard_map/while/body/eval_jaxpr/ppermute | solution.py:9
  909.3 127.4 %reduce-scatter.2.cloned.1.call-start = ((), (), s32[]{:S(2)}) async-start(), calls=%async_computation.1 | async-start | bytes 1081344 | tf_op jit(solution)/shard_map/while/body/eval_jaxpr/reduce_scatter | solution.py:35
  919.8 117.6 %collective-permute-start = (bf16[1536,512]{1,0:T(8,128)(2,1)S(1)}, bf16[1536,512]{1,0:T(8,128)(2,1)S(1)}, u32[]{:S(2)}, u32[]{:S(2)}) collective-permute-start(bf16[1536,512]{1,0:T(8,128)(2,1)S(1)} %copy.10), channel_id=1, source_target_pairs={{0,32},{32,64},{64,96},{96,128},{128,160},{160,192},{192,224},{224... | collective-permute-start | bytes 4718600 | tf_op jit(solution)/shard_map/while/body/eval_jaxpr/ppermute | solution.py:9
Sparse Core Ops, SparseCore 0:
  18.6 119.8 reduce-scatter.1
  149.9 116.9 reduce-scatter.1
  278.3 116.9 reduce-scatter.1
  406.7 116.6 reduce-scatter.1
  534.8 116.9 reduce-scatter.1
  663.2 117.0 reduce-scatter.1
  791.7 116.7 reduce-scatter.1
  919.9 116.6 reduce-scatter.1
